TPU v7x, 512 devices: a whole 4x4x16 slice. The times are simulated.
512 devices in a mesh: row: 16 (over y_hi, x, core), col: 32 (over y_lo, z).
Axes of the slice: x: 4, y: 4 (y_hi: 2, y_lo: 2; y = y_hi * 2 + y_lo), z: 16, core: 2. Of those that a mesh axis runs over, the one named last changes fastest.
Arguments:
- inputs: bfloat16 [512, 8192], P('col', 'row'), may hold values from -6 to 6
- out_grad: bfloat16 [512, 8192], P('col', 'row'), may hold values from -0.8984375 to 0.8984375
- gate_pre: bfloat16 [512, 16384], P('row', 'col'), may hold values from -6 to 6
- up_pre: bfloat16 [512, 16384], P('row', 'col'), may hold values from -6 to 6
- gate_weight: bfloat16 [8192, 16384], P('row', 'col'), may hold values from -0.0625 to 0.0625
- up_weight: bfloat16 [8192, 16384], P('row', 'col'), may hold values from -0.0625 to 0.0625
- down_weight: bfloat16 [16384, 8192], P('col', 'row'), may hold values from -0.0625 to 0.0625
Outputs:
- input_grad: bfloat16 [512, 8192], P('col', 'row')
- gate_grad: bfloat16 [8192, 16384], P('row', 'col')
- up_grad: bfloat16 [8192, 16384], P('row', 'col')
- down_grad: bfloat16 [16384, 8192], P('col', 'row')
All inputs are finite; a program needn't handle non-finite values.
Results may differ from a plain program's by a relative error of at most 0.028.
Values may be sent and summed in bfloat16 or wider, within the bound.
No kernel may reach another device: no remote copies, remote signals or barrier semaphores. Data moves between devices by JAX's collectives and lax.ppermute only.
A program may use at most 64 MiB of HBM per device.

v0:
```python
import jax
import jax.numpy as jnp
from jax import lax
from jax.sharding import Mesh
from jax.sharding import PartitionSpec as P

GRID = ("y_hi", "x_hi", "x_lo", "core")
ROW = ("core", "y_hi", "x_hi", "x_lo")
PLANE = ("y_hi", "x_hi", "x_lo")
COL = ("y_lo", "z3", "z2", "z1", "z_lo")
NEAR = ("y_lo", "z_lo")
FAR = ("z3", "z2", "z1")


def product(x, y, contract):
    return lax.dot_general(
        x, y, (((contract,), (contract,)), ((), ())), preferred_element_type=jnp.float32
    )


def exchanged(blocks, axes):
    return lax.all_to_all(blocks, axes, 0, 0, tiled=True)


def sent_to_all(array, axes):
    peers = lax.axis_size(axes)
    return exchanged(jnp.broadcast_to(array[None], (peers, *array.shape)), axes)


def summed(blocks):
    return blocks.astype(jnp.float32).sum(axis=0)


def far_gathered(out_grad, inputs):
    first = lax.broadcasted_iota(jnp.int32, (lax.axis_size(FAR), 2, 1, 1), 1) == 0
    far = exchanged(jnp.where(first, out_grad, inputs), FAR)
    return far[:, 0], far[:, 1]


def grads_gathered(far):
    return sent_to_all(far, NEAR).reshape(-1, far.shape[2])


def doubled(array, axis, place):
    other = lax.ppermute(array, axis, ((0, 1), (1, 0)))
    second = lax.axis_index(axis) == 1
    return jnp.stack((jnp.where(second, other, array), jnp.where(second, array, other)), axis=place)


def inputs_gathered(far):
    blocks = doubled(far, "z_lo", 0)
    blocks = doubled(blocks, "y_lo", 0)
    return blocks.reshape(-1, far.shape[2])


def pre_gathered(gate_pre, up_pre):
    _, width = gate_pre.shape
    blocks = jnp.stack((gate_pre, up_pre)).reshape(2, lax.axis_size("z_lo"), -1, width)
    blocks = doubled(blocks, "y_hi", 1)
    blocks = doubled(blocks, "x_hi", 3)
    blocks = doubled(blocks, "x_lo", 4)
    blocks = doubled(blocks, "core", 5)
    return lax.optimization_barrier((blocks[0].reshape(-1, width), blocks[1].reshape(-1, width)))


def hidden_sum(partial):
    width = partial.shape[1]
    blocks = partial.reshape(lax.axis_size(ROW), -1, width)
    share = summed(exchanged(blocks, ROW)).astype(jnp.bfloat16)
    plane = sent_to_all(share, PLANE)
    return lax.all_gather(plane, "core").reshape(-1, width)


def near_sum(partial, tokens):
    blocks = partial.reshape(lax.axis_size(NEAR), -1, tokens, partial.shape[1])
    return summed(exchanged(blocks, NEAR)).astype(jnp.bfloat16)


def far_sum(blocks):
    return summed(exchanged(blocks, FAR)).astype(jnp.bfloat16)


def hidden_of(pre):
    gate, up = pre[0].astype(jnp.float32), pre[1].astype(jnp.float32)
    return (gate / (1.0 + jnp.exp(-gate)) * up).astype(jnp.bfloat16)


def deltas(pre, hidden_grad):
    gate, up = pre[0].astype(jnp.float32), pre[1].astype(jnp.float32)
    grad = hidden_grad.astype(jnp.float32)
    sigmoid = 1.0 / (1.0 + jnp.exp(-gate))
    gate_delta = grad * up * sigmoid * (1.0 + gate * (1.0 - sigmoid))
    return gate_delta.astype(jnp.bfloat16), (grad * (gate * sigmoid)).astype(jnp.bfloat16)


def per_device(inputs, out_grad, gate_pre, up_pre, gate_weight, up_weight, down_weight):
    bf16 = jnp.bfloat16
    far_grads, far_inputs = far_gathered(out_grad, inputs)
    all_grads = grads_gathered(far_grads)
    all_inputs = inputs_gathered(far_inputs)
    pre = pre_gathered(gate_pre, up_pre)
    hidden, *pre = lax.optimization_barrier((hidden_of(pre), *pre))
    hidden_grad = hidden_sum(product(all_grads, down_weight, 1).astype(bf16))
    gate_delta, up_delta = lax.optimization_barrier(deltas(pre, hidden_grad))
    partial = product(gate_delta, gate_weight, 1) + product(up_delta, up_weight, 1)
    near = near_sum(partial.astype(bf16), inputs.shape[0])
    input_grad = far_sum(near)
    down_grad = product(hidden, all_grads, 0).astype(bf16)
    gate_grad = product(all_inputs, gate_delta, 0).astype(bf16)
    up_grad = product(all_inputs, up_delta, 0).astype(bf16)
    return input_grad, gate_grad, up_grad, down_grad


def solution(mesh):
    split = Mesh(mesh.devices.reshape(2, 2, 2, 2, 2, 2, 2, 2, 2), GRID + COL)
    tokens_by_col, tokens_by_row = P(COL, GRID), P(GRID, COL)
    in_specs = (
        tokens_by_col,
        tokens_by_col,
        tokens_by_row,
        tokens_by_row,
        tokens_by_row,
        tokens_by_row,
        tokens_by_col,
    )
    out_specs = (tokens_by_col, tokens_by_row, tokens_by_row, tokens_by_col)
    return jax.shard_map(
        per_device, mesh=split, in_specs=in_specs, out_specs=out_specs, check_vma=False
    )
```

profile of v0, /device:TPU:2, one launch (start us, length us, event | category | flops | bytes accessed | tf_op | source)
XLA Modules:
  0.0 148.8 jit_solution(16946979855672164500)
XLA Ops:
  0.6 0.0 copy-start
  0.7 1.6 %broadcast_select_fusion = bf16[8,2,16,512]{3,2,1,0:T(8,128)(2,1)} fusion(pred[2]{0:T(512)(128)(4,1)S(1)} %iota_compare_fusion, bf16[16,512]{1,0:T(8,128)(2,1)} %param.7, bf16[16,512]{1,0:T(8,128)(2,1)} %param.8), kind=kLoop, calls=%fused_computation.39 | loop fusion | flops 131072 | bytes 294914 | tf_op jit(solution)/shard_map/jit(_where)/select_n | solution.py:36
  2.2 15.2 %all-to-all-start = ((bf16[8,2,16,512]{3,2,1,0:T(8,128)(2,1)}), bf16[8,2,16,512]{3,2,1,0:T(8,128)(2,1)S(1)}, u32[]{:S(2)}, u32[]{:S(2)}) async-start(bf16[8,2,16,512]{3,2,1,0:T(8,128)(2,1)} %broadcast_select_fusion), calls=%async_computation | async-start | bytes 524288 | tf_op jit(solution)/shard_map/all_to_all | solution.py:22
  17.5 5.1 %collective-permute-start = (bf16[2,2,16,512]{3,2,1,0:T(8,128)(2,1)S(1)}, bf16[2,2,16,512]{3,2,1,0:T(8,128)(2,1)S(1)}, u32[]{:S(2)}, u32[]{:S(2)}) collective-permute-start(bf16[2,2,16,512]{3,2,1,0:T(8,128)(2,1)S(1)} %pad_maximum_fusion.6), channel_id=1, source_target_pairs={{0,256},{256,0},{1,257},{257,1},{2,258},{258,2},{3,259},{259,3},{4... | collective-permute-start | bytes 196616 | tf_op jit(solution)/shard_map/ppermute | solution.py:45
  22.6 16.2 %all-to-all-done = bf16[8,2,16,512]{3,2,1,0:T(8,128)(2,1)S(1)} async-done(((bf16[8,2,16,512]{3,2,1,0:T(8,128)(2,1)}), bf16[8,2,16,512]{3,2,1,0:T(8,128)(2,1)S(1)}, u32[]{:S(2)}, u32[]{:S(2)}) %all-to-all-start) | async-done | bytes 262176 | tf_op jit(solution)/shard_map/all_to_all | solution.py:22
  38.9 0.9 broadcast_in_dim.33
  39.7 3.5 %all-to-all-start.1 = ((bf16[4,8,16,512]{3,2,1,0:T(8,128)(2,1)}), bf16[4,8,16,512]{3,2,1,0:T(8,128)(2,1)S(1)}, u32[]{:S(2)}, u32[]{:S(2)}) async-start(bf16[4,8,16,512]{3,2,1,0:T(8,128)(2,1)} %broadcast_in_dim.33), calls=%async_computation.1 | async-start | bytes 1048576 | tf_op jit(solution)/shard_map/all_to_all | solution.py:22
  43.2 0.0 collective-permute-done
  43.2 4.0 %collective-permute-start.1 = (bf16[2,2,2,16,512]{4,3,2,1,0:T(8,128)(2,1)S(1)}, bf16[2,2,2,16,512]{4,3,2,1,0:T(8,128)(2,1)S(1)}, u32[]{:S(2)}, u32[]{:S(2)}) collective-permute-start(bf16[2,2,2,16,512]{4,3,2,1,0:T(8,128)(2,1)S(1)} %pad_maximum_fusion.5), channel_id=1, source_target_pairs={{0,128},{128,0},{1,129},{129,1},{2,130},{130,2},{3,131},{131,3},{4... | collective-permute-start | bytes 393224 | tf_op jit(solution)/shard_map/ppermute | solution.py:45
  47.3 4.5 %collective-permute-done.1 = bf16[2,2,2,16,512]{4,3,2,1,0:T(8,128)(2,1)S(1)} collective-permute-done((bf16[2,2,2,16,512]{4,3,2,1,0:T(8,128)(2,1)S(1)}, bf16[2,2,2,16,512]{4,3,2,1,0:T(8,128)(2,1)S(1)}, u32[]{:S(2)}, u32[]{:S(2)}) %collective-permute-start.1) | collective-permute-done | bytes 131104 | tf_op jit(solution)/shard_map/ppermute | solution.py:45
  51.9 2.4 %collective-permute-start.2 = (bf16[2,2,2,2,16,512]{5,4,3,2,1,0:T(8,128)(2,1)S(1)}, bf16[2,2,2,2,16,512]{5,4,3,2,1,0:T(8,128)(2,1)S(1)}, u32[]{:S(2)}, u32[]{:S(2)}) collective-permute-start(bf16[2,2,2,2,16,512]{5,4,3,2,1,0:T(8,128)(2,1)S(1)} %pad_maximum_fusion.3), channel_id=1, source_target_pairs={{0,64},{64,0},{1,65},{65,1},{2,66},{66,2},{3,67},{67,3},{4,68},{68... | collective-permute-start | bytes 786440 | tf_op jit(solution)/shard_map/ppermute | solution.py:45
  54.3 5.8 %collective-permute-done.2 = bf16[2,2,2,2,16,512]{5,4,3,2,1,0:T(8,128)(2,1)S(1)} collective-permute-done((bf16[2,2,2,2,16,512]{5,4,3,2,1,0:T(8,128)(2,1)S(1)}, bf16[2,2,2,2,16,512]{5,4,3,2,1,0:T(8,128)(2,1)S(1)}, u32[]{:S(2)}, u32[]{:S(2)}) %collective-permute-start.2) | collective-permute-done | bytes 262176 | tf_op jit(solution)/shard_map/ppermute | solution.py:45
  60.2 0.1 pad_maximum_fusion.1
  60.3 1.9 %collective-permute-start.3 = (bf16[2,2,2,2,2,16,512]{6,5,4,3,2,1,0:T(8,128)(2,1)S(1)}, bf16[2,2,2,2,2,16,512]{6,5,4,3,2,1,0:T(8,128)(2,1)S(1)}, u32[]{:S(2)}, u32[]{:S(2)}) collective-permute-start(bf16[2,2,2,2,2,16,512]{6,5,4,3,2,1,0:T(8,128)(2,1)S(1)} %pad_maximum_fusion.1), channel_id=1, source_target_pairs={{0,32},{32,0},{1,33},{33,1},{2,34},{34,2},{3,35},{35,3},{4,36},{36... | collective-permute-start | bytes 1572872 | tf_op jit(solution)/shard_map/ppermute | solution.py:45
  62.2 0.0 all-to-all-done.1
  62.2 1.3 convolution_convert_fusion.3
  63.5 8.5 %all-to-all-start.2 = ((bf16[16,32,512]{2,1,0:T(8,128)(2,1)}), bf16[16,32,512]{2,1,0:T(8,128)(2,1)S(1)}, u32[]{:S(2)}, u32[]{:S(2)}) async-start(bf16[16,32,512]{2,1,0:T(8,128)(2,1)} %bitcast.2), calls=%async_computation.2 | async-start | bytes 1048576 | tf_op jit(solution)/shard_map/all_to_all | solution.py:22
  72.0 0.0 collective-permute-done.3
  72.0 0.1 select_bitcast_fusion
  72.1 0.1 pad_maximum_fusion
  72.2 10.5 %all-to-all-done.2 = bf16[16,32,512]{2,1,0:T(8,128)(2,1)S(1)} async-done(((bf16[16,32,512]{2,1,0:T(8,128)(2,1)}), bf16[16,32,512]{2,1,0:T(8,128)(2,1)S(1)}, u32[]{:S(2)}, u32[]{:S(2)}) %all-to-all-start.2) | async-done | bytes 524320 | tf_op jit(solution)/shard_map/all_to_all | solution.py:22
  82.7 0.1 reduce_sum.36
  82.8 0.7 broadcast_in_dim.34
  83.5 4.8 %all-to-all-start.3 = ((bf16[8,32,512]{2,1,0:T(8,128)(2,1)}), bf16[8,32,512]{2,1,0:T(8,128)(2,1)S(1)}, u32[]{:S(2)}, u32[]{:S(2)}) async-start(bf16[8,32,512]{2,1,0:T(8,128)(2,1)} %broadcast_in_dim.34), calls=%async_computation.3 | async-start | bytes 524288 | tf_op jit(solution)/shard_map/all_to_all | solution.py:22
  88.3 1.1 fusion.12
  89.5 7.4 %all-to-all-done.3 = bf16[8,32,512]{2,1,0:T(8,128)(2,1)S(1)} async-done(((bf16[8,32,512]{2,1,0:T(8,128)(2,1)}), bf16[8,32,512]{2,1,0:T(8,128)(2,1)S(1)}, u32[]{:S(2)}, u32[]{:S(2)}) %all-to-all-start.3) | async-done | bytes 262176 | tf_op jit(solution)/shard_map/all_to_all | solution.py:22
  96.8 2.2 %all-gather = bf16[16,32,512]{2,1,0:T(8,128)(2,1)S(1)} all-gather(bf16[8,32,512]{2,1,0:T(8,128)(2,1)S(1)} %all-to-all-done.3), channel_id=2, replica_groups=mesh['y_hi'=2,'x_hi'=2,'x_lo'=2,'core'=2,'y_lo'=2,'z3'=2,'z2'=2,'z1'=2,'..., dimensions={0}, use_global_device_ids=true | all-gather | bytes 786432 | tf_op jit(solution)/shard_map/all_gather | solution.py:71
  99.0 0.6 fusion.7
  99.6 0.4 copy-done.4
  100.0 0.5 fusion.14
  100.5 0.6 copy-done.1
  101.1 1.3 fusion
  102.3 3.8 %all-to-all-start.4 = ((bf16[4,8,16,512]{3,2,1,0:T(8,128)(2,1)}), bf16[4,8,16,512]{3,2,1,0:T(8,128)(2,1)S(1)}, u32[]{:S(2)}, u32[]{:S(2)}) async-start(bf16[4,8,16,512]{3,2,1,0:T(8,128)(2,1)} %bitcast.21), calls=%async_computation.4 | async-start | bytes 1048576 | tf_op jit(solution)/shard_map/all_to_all | solution.py:22
  106.1 3.9 %collective-permute-start.4 = (bf16[8,16,512]{2,1,0:T(8,128)(2,1)S(1)}, bf16[8,16,512]{2,1,0:T(8,128)(2,1)S(1)}, u32[]{:S(2)}, u32[]{:S(2)}) collective-permute-start(bf16[8,16,512]{2,1,0:T(8,128)(2,1)S(1)} %get-tuple-element.30), channel_id=1, source_target_pairs={{0,1},{1,0},{2,3},{3,2},{4,5},{5,4},{6,7},{7,6},{8,9},{9,8},{10,11... | collective-permute-start | bytes 393224 | tf_op jit(solution)/shard_map/ppermute | solution.py:45
  110.0 7.6 %collective-permute-done.4 = bf16[8,16,512]{2,1,0:T(8,128)(2,1)S(1)} collective-permute-done((bf16[8,16,512]{2,1,0:T(8,128)(2,1)S(1)}, bf16[8,16,512]{2,1,0:T(8,128)(2,1)S(1)}, u32[]{:S(2)}, u32[]{:S(2)}) %collective-permute-start.4) | collective-permute-done | bytes 131104 | tf_op jit(solution)/shard_map/ppermute | solution.py:45
  117.7 3.0 %collective-permute-start.5 = (bf16[2,8,16,512]{3,2,1,0:T(8,128)(2,1)S(1)}, bf16[2,8,16,512]{3,2,1,0:T(8,128)(2,1)S(1)}, u32[]{:S(2)}, u32[]{:S(2)}) collective-permute-start(bf16[2,8,16,512]{3,2,1,0:T(8,128)(2,1)S(1)} %pad_maximum_fusion.4), channel_id=1, source_target_pairs={{0,16},{16,0},{1,17},{17,1},{2,18},{18,2},{3,19},{19,3},{4,20},{20... | collective-permute-start | bytes 786440 | tf_op jit(solution)/shard_map/ppermute | solution.py:45
  120.7 6.6 %collective-permute-done.5 = bf16[2,8,16,512]{3,2,1,0:T(8,128)(2,1)S(1)} collective-permute-done((bf16[2,8,16,512]{3,2,1,0:T(8,128)(2,1)S(1)}, bf16[2,8,16,512]{3,2,1,0:T(8,128)(2,1)S(1)}, u32[]{:S(2)}, u32[]{:S(2)}) %collective-permute-start.5) | collective-permute-done | bytes 262176 | tf_op jit(solution)/shard_map/ppermute | solution.py:45
  127.3 0.0 copy-start.2
  127.3 0.8 pad_maximum_fusion.2
  128.1 0.4 copy-done.2
  128.5 1.3 convolution_convert_fusion
  129.8 0.0 all-to-all-done.4
  129.8 0.7 reduce_sum.37
  130.5 3.4 %all-to-all-start.5 = ((bf16[8,16,512]{2,1,0:T(8,128)(2,1)}), bf16[8,16,512]{2,1,0:T(8,128)(2,1)S(1)}, u32[]{:S(2)}, u32[]{:S(2)}) async-start(bf16[8,16,512]{2,1,0:T(8,128)(2,1)} %reduce_sum.37), calls=%async_computation.5 | async-start | bytes 262144 | tf_op jit(solution)/shard_map/all_to_all | solution.py:22
  133.9 1.3 convolution_convert_fusion.2
  135.2 1.3 convolution_convert_fusion.1
  136.4 11.8 %all-to-all-done.5 = bf16[8,16,512]{2,1,0:T(8,128)(2,1)S(1)} async-done(((bf16[8,16,512]{2,1,0:T(8,128)(2,1)}), bf16[8,16,512]{2,1,0:T(8,128)(2,1)S(1)}, u32[]{:S(2)}, u32[]{:S(2)}) %all-to-all-start.5) | async-done | bytes 131104 | tf_op jit(solution)/shard_map/all_to_all | solution.py:22
  148.2 0.6 reduce_sum.38
  (20 shorter events, 0.3 us)
Async XLA Ops:
  0.6 61.6 %copy-start = (bf16[512,512]{1,0:T(8,128)(2,1)S(1)}, bf16[512,512]{1,0:T(8,128)(2,1)}, u32[]{:S(2)}) copy-start(bf16[512,512]{1,0:T(8,128)(2,1)} %param.13) | copy-start | bytes 1572868
  2.2 15.2 %copy-start.5 = (bf16[32,512]{1,0:T(8,128)(2,1)S(1)}, bf16[32,512]{1,0:T(8,128)(2,1)}, u32[]{:S(2)}) copy-start(bf16[32,512]{1,0:T(8,128)(2,1)} %param.10) | copy-start | bytes 98308
  2.2 15.2 %copy-start.6 = (bf16[32,512]{1,0:T(8,128)(2,1)S(1)}, bf16[32,512]{1,0:T(8,128)(2,1)}, u32[]{:S(2)}) copy-start(bf16[32,512]{1,0:T(8,128)(2,1)} %param.9) | copy-start | bytes 98308
  2.2 36.6 %all-to-all-start = ((bf16[8,2,16,512]{3,2,1,0:T(8,128)(2,1)}), bf16[8,2,16,512]{3,2,1,0:T(8,128)(2,1)S(1)}, u32[]{:S(2)}, u32[]{:S(2)}) async-start(bf16[8,2,16,512]{3,2,1,0:T(8,128)(2,1)} %broadcast_select_fusion), calls=%async_computation | async-start | bytes 524288 | tf_op jit(solution)/shard_map/all_to_all | solution.py:22
  17.5 25.7 %collective-permute-start = (bf16[2,2,16,512]{3,2,1,0:T(8,128)(2,1)S(1)}, bf16[2,2,16,512]{3,2,1,0:T(8,128)(2,1)S(1)}, u32[]{:S(2)}, u32[]{:S(2)}) collective-permute-start(bf16[2,2,16,512]{3,2,1,0:T(8,128)(2,1)S(1)} %pad_maximum_fusion.6), channel_id=1, source_target_pairs={{0,256},{256,0},{1,257},{257,1},{2,258},{258,2},{3,259},{259,3},{4... | collective-permute-start | bytes 196616 | tf_op jit(solution)/shard_map/ppermute | solution.py:45
  39.7 22.5 %all-to-all-start.1 = ((bf16[4,8,16,512]{3,2,1,0:T(8,128)(2,1)}), bf16[4,8,16,512]{3,2,1,0:T(8,128)(2,1)S(1)}, u32[]{:S(2)}, u32[]{:S(2)}) async-start(bf16[4,8,16,512]{3,2,1,0:T(8,128)(2,1)} %broadcast_in_dim.33), calls=%async_computation.1 | async-start | bytes 1048576 | tf_op jit(solution)/shard_map/all_to_all | solution.py:22
  43.2 8.6 %collective-permute-start.1 = (bf16[2,2,2,16,512]{4,3,2,1,0:T(8,128)(2,1)S(1)}, bf16[2,2,2,16,512]{4,3,2,1,0:T(8,128)(2,1)S(1)}, u32[]{:S(2)}, u32[]{:S(2)}) collective-permute-start(bf16[2,2,2,16,512]{4,3,2,1,0:T(8,128)(2,1)S(1)} %pad_maximum_fusion.5), channel_id=1, source_target_pairs={{0,128},{128,0},{1,129},{129,1},{2,130},{130,2},{3,131},{131,3},{4... | collective-permute-start | bytes 393224 | tf_op jit(solution)/shard_map/ppermute | solution.py:45
  51.9 8.3 %collective-permute-start.2 = (bf16[2,2,2,2,16,512]{5,4,3,2,1,0:T(8,128)(2,1)S(1)}, bf16[2,2,2,2,16,512]{5,4,3,2,1,0:T(8,128)(2,1)S(1)}, u32[]{:S(2)}, u32[]{:S(2)}) collective-permute-start(bf16[2,2,2,2,16,512]{5,4,3,2,1,0:T(8,128)(2,1)S(1)} %pad_maximum_fusion.3), channel_id=1, source_target_pairs={{0,64},{64,0},{1,65},{65,1},{2,66},{66,2},{3,67},{67,3},{4,68},{68... | collective-permute-start | bytes 786440 | tf_op jit(solution)/shard_map/ppermute | solution.py:45
  60.3 11.8 %collective-permute-start.3 = (bf16[2,2,2,2,2,16,512]{6,5,4,3,2,1,0:T(8,128)(2,1)S(1)}, bf16[2,2,2,2,2,16,512]{6,5,4,3,2,1,0:T(8,128)(2,1)S(1)}, u32[]{:S(2)}, u32[]{:S(2)}) collective-permute-start(bf16[2,2,2,2,2,16,512]{6,5,4,3,2,1,0:T(8,128)(2,1)S(1)} %pad_maximum_fusion.1), channel_id=1, source_target_pairs={{0,32},{32,0},{1,33},{33,1},{2,34},{34,2},{3,35},{35,3},{4,36},{36... | collective-permute-start | bytes 1572872 | tf_op jit(solution)/shard_map/ppermute | solution.py:45
  63.5 19.3 %all-to-all-start.2 = ((bf16[16,32,512]{2,1,0:T(8,128)(2,1)}), bf16[16,32,512]{2,1,0:T(8,128)(2,1)S(1)}, u32[]{:S(2)}, u32[]{:S(2)}) async-start(bf16[16,32,512]{2,1,0:T(8,128)(2,1)} %bitcast.2), calls=%async_computation.2 | async-start | bytes 1048576 | tf_op jit(solution)/shard_map/all_to_all | solution.py:22
  83.5 13.3 %all-to-all-start.3 = ((bf16[8,32,512]{2,1,0:T(8,128)(2,1)}), bf16[8,32,512]{2,1,0:T(8,128)(2,1)S(1)}, u32[]{:S(2)}, u32[]{:S(2)}) async-start(bf16[8,32,512]{2,1,0:T(8,128)(2,1)} %broadcast_in_dim.34), calls=%async_computation.3 | async-start | bytes 524288 | tf_op jit(solution)/shard_map/all_to_all | solution.py:22
  99.0 1.0 copy-start.4
  100.0 1.0 copy-start.1
  102.3 27.5 %all-to-all-start.4 = ((bf16[4,8,16,512]{3,2,1,0:T(8,128)(2,1)}), bf16[4,8,16,512]{3,2,1,0:T(8,128)(2,1)S(1)}, u32[]{:S(2)}, u32[]{:S(2)}) async-start(bf16[4,8,16,512]{3,2,1,0:T(8,128)(2,1)} %bitcast.21), calls=%async_computation.4 | async-start | bytes 1048576 | tf_op jit(solution)/shard_map/all_to_all | solution.py:22
  106.1 11.5 %collective-permute-start.4 = (bf16[8,16,512]{2,1,0:T(8,128)(2,1)S(1)}, bf16[8,16,512]{2,1,0:T(8,128)(2,1)S(1)}, u32[]{:S(2)}, u32[]{:S(2)}) collective-permute-start(bf16[8,16,512]{2,1,0:T(8,128)(2,1)S(1)} %get-tuple-element.30), channel_id=1, source_target_pairs={{0,1},{1,0},{2,3},{3,2},{4,5},{5,4},{6,7},{7,6},{8,9},{9,8},{10,11... | collective-permute-start | bytes 393224 | tf_op jit(solution)/shard_map/ppermute | solution.py:45
  117.7 9.5 %collective-permute-start.5 = (bf16[2,8,16,512]{3,2,1,0:T(8,128)(2,1)S(1)}, bf16[2,8,16,512]{3,2,1,0:T(8,128)(2,1)S(1)}, u32[]{:S(2)}, u32[]{:S(2)}) collective-permute-start(bf16[2,8,16,512]{3,2,1,0:T(8,128)(2,1)S(1)} %pad_maximum_fusion.4), channel_id=1, source_target_pairs={{0,16},{16,0},{1,17},{17,1},{2,18},{18,2},{3,19},{19,3},{4,20},{20... | collective-permute-start | bytes 786440 | tf_op jit(solution)/shard_map/ppermute | solution.py:45
  127.3 1.2 copy-start.2
  129.8 4.1 %copy-start.3 = (bf16[2,2,8,16,512]{4,3,2,1,0:T(8,128)(2,1)S(1)}, bf16[2,2,8,16,512]{4,3,2,1,0:T(8,128)(2,1)}, u32[]{:S(2)}) copy-start(bf16[2,2,8,16,512]{4,3,2,1,0:T(8,128)(2,1)} %pad_maximum_fusion.2) | copy-start | bytes 1572868
  130.5 17.7 %all-to-all-start.5 = ((bf16[8,16,512]{2,1,0:T(8,128)(2,1)}), bf16[8,16,512]{2,1,0:T(8,128)(2,1)S(1)}, u32[]{:S(2)}, u32[]{:S(2)}) async-start(bf16[8,16,512]{2,1,0:T(8,128)(2,1)} %reduce_sum.37), calls=%async_computation.5 | async-start | bytes 262144 | tf_op jit(solution)/shard_map/all_to_all | solution.py:22
where the time goes:
time: 150 us; the launch traced here: 149 us
  waiting for transfers between devices  70.5 us (47%)
  starting transfers between devices  59.5 us (40%)
  matrix products  6.77 us (5%)
  other arithmetic  6.03 us (4%)
  local copies, waits for them, and re-layouts  3.01 us (2%)
  blocking collectives  2.17 us (1%)
    all_to_all x6, waiting for transfers between devices, exchanged(): return lax.all_to_all(blocks, axes, 0, 0, tiled=True)  45.9 us
    all_to_all x6, starting transfers between devices, exchanged(): return lax.all_to_all(blocks, axes, 0, 0, tiled=True)  39.1 us
    ppermute x6, waiting for transfers between devices, doubled(): other = lax.ppermute(array, axis, ((0, 1), (1, 0)))  24.5 us
    ppermute x6, starting transfers between devices, doubled(): other = lax.ppermute(array, axis, ((0, 1), (1, 0)))  20.4 us
    dot_general x6, matrix products, product(): lax.dot_general(x, y, (((contract,), (contract,)), ((), ())), preferred_e...  6.77 us
  transfers between devices with their start and end apart: 12, of which 8 were waited for; matrix products, arithmetic and copies ran while one was open for 6% of the time, Pallas kernels for 0%

commit v1 on v0

--- a/solution.py
+++ b/solution.py
@@ -44,7 +44,9 @@
 def doubled(array, axis, place):
     other = lax.ppermute(array, axis, ((0, 1), (1, 0)))
     second = lax.axis_index(axis) == 1
-    return jnp.stack((jnp.where(second, other, array), jnp.where(second, array, other)), axis=place)
+    return jnp.stack(
+        (jnp.where(second, other, array), jnp.where(second, array, other)), axis=place
+    )
 
 
 def inputs_gathered(far):
@@ -60,7 +62,7 @@
     blocks = doubled(blocks, "x_hi", 3)
     blocks = doubled(blocks, "x_lo", 4)
     blocks = doubled(blocks, "core", 5)
-    return lax.optimization_barrier((blocks[0].reshape(-1, width), blocks[1].reshape(-1, width)))
+    return blocks[0].reshape(-1, width), blocks[1].reshape(-1, width)
 
 
 def hidden_sum(partial):

time: 150 us -> 150 us (level)
  no operation moved by 1% of the time
where the time goes in v1:
time: 150 us; the launch traced here: 149 us
  waiting for transfers between devices  70.4 us (47%)
  starting transfers between devices  59.5 us (40%)
  matrix products  6.77 us (5%)
  other arithmetic  6.1 us (4%)
  local copies, waits for them, and re-layouts  3.01 us (2%)
  blocking collectives  2.17 us (1%)
    all_to_all x6, waiting for transfers between devices, exchanged(): return lax.all_to_all(blocks, axes, 0, 0, tiled=True)  45.9 us
    all_to_all x6, starting transfers between devices, exchanged(): return lax.all_to_all(blocks, axes, 0, 0, tiled=True)  39.1 us
    ppermute x6, waiting for transfers between devices, doubled(): other = lax.ppermute(array, axis, ((0, 1), (1, 0)))  24.5 us
    ppermute x6, starting transfers between devices, doubled(): other = lax.ppermute(array, axis, ((0, 1), (1, 0)))  20.4 us
    dot_general x6, matrix products, product(): lax.dot_general(x, y, (((contract,), (contract,)), ((), ())), preferred_e...  6.77 us
  transfers between devices with their start and end apart: 12, of which 8 were waited for; matrix products, arithmetic and copies ran while one was open for 6% of the time, Pallas kernels for 0%

profile of v1, /device:TPU:2, one launch (start us, length us, event | category | flops | bytes accessed | tf_op | source)
XLA Modules:
  0.0 148.8 jit_solution(665177895304168265)
XLA Ops:
  0.6 0.0 copy-start
  0.7 1.6 %broadcast_select_fusion = bf16[8,2,16,512]{3,2,1,0:T(8,128)(2,1)} fusion(pred[2]{0:T(512)(128)(4,1)S(1)} %iota_compare_fusion, bf16[16,512]{1,0:T(8,128)(2,1)} %param.7, bf16[16,512]{1,0:T(8,128)(2,1)} %param.8), kind=kLoop, calls=%fused_computation.39 | loop fusion | flops 131072 | bytes 294914 | tf_op jit(solution)/shard_map/jit(_where)/select_n | solution.py:36
  2.2 15.2 %all-to-all-start = ((bf16[8,2,16,512]{3,2,1,0:T(8,128)(2,1)}), bf16[8,2,16,512]{3,2,1,0:T(8,128)(2,1)S(1)}, u32[]{:S(2)}, u32[]{:S(2)}) async-start(bf16[8,2,16,512]{3,2,1,0:T(8,128)(2,1)} %broadcast_select_fusion), calls=%async_computation | async-start | bytes 524288 | tf_op jit(solution)/shard_map/all_to_all | solution.py:22
  17.5 5.1 %collective-permute-start = (bf16[2,2,16,512]{3,2,1,0:T(8,128)(2,1)S(1)}, bf16[2,2,16,512]{3,2,1,0:T(8,128)(2,1)S(1)}, u32[]{:S(2)}, u32[]{:S(2)}) collective-permute-start(bf16[2,2,16,512]{3,2,1,0:T(8,128)(2,1)S(1)} %pad_maximum_fusion.6), channel_id=1, source_target_pairs={{0,256},{256,0},{1,257},{257,1},{2,258},{258,2},{3,259},{259,3},{4... | collective-permute-start | bytes 196616 | tf_op jit(solution)/shard_map/ppermute | solution.py:45
  22.6 16.2 %all-to-all-done = bf16[8,2,16,512]{3,2,1,0:T(8,128)(2,1)S(1)} async-done(((bf16[8,2,16,512]{3,2,1,0:T(8,128)(2,1)}), bf16[8,2,16,512]{3,2,1,0:T(8,128)(2,1)S(1)}, u32[]{:S(2)}, u32[]{:S(2)}) %all-to-all-start) | async-done | bytes 262176 | tf_op jit(solution)/shard_map/all_to_all | solution.py:22
  38.9 0.9 broadcast_in_dim.33
  39.7 3.5 %all-to-all-start.1 = ((bf16[4,8,16,512]{3,2,1,0:T(8,128)(2,1)}), bf16[4,8,16,512]{3,2,1,0:T(8,128)(2,1)S(1)}, u32[]{:S(2)}, u32[]{:S(2)}) async-start(bf16[4,8,16,512]{3,2,1,0:T(8,128)(2,1)} %broadcast_in_dim.33), calls=%async_computation.1 | async-start | bytes 1048576 | tf_op jit(solution)/shard_map/all_to_all | solution.py:22
  43.2 0.0 collective-permute-done
  43.2 4.0 %collective-permute-start.1 = (bf16[2,2,2,16,512]{4,3,2,1,0:T(8,128)(2,1)S(1)}, bf16[2,2,2,16,512]{4,3,2,1,0:T(8,128)(2,1)S(1)}, u32[]{:S(2)}, u32[]{:S(2)}) collective-permute-start(bf16[2,2,2,16,512]{4,3,2,1,0:T(8,128)(2,1)S(1)} %pad_maximum_fusion.5), channel_id=1, source_target_pairs={{0,128},{128,0},{1,129},{129,1},{2,130},{130,2},{3,131},{131,3},{4... | collective-permute-start | bytes 393224 | tf_op jit(solution)/shard_map/ppermute | solution.py:45
  47.3 4.5 %collective-permute-done.1 = bf16[2,2,2,16,512]{4,3,2,1,0:T(8,128)(2,1)S(1)} collective-permute-done((bf16[2,2,2,16,512]{4,3,2,1,0:T(8,128)(2,1)S(1)}, bf16[2,2,2,16,512]{4,3,2,1,0:T(8,128)(2,1)S(1)}, u32[]{:S(2)}, u32[]{:S(2)}) %collective-permute-start.1) | collective-permute-done | bytes 131104 | tf_op jit(solution)/shard_map/ppermute | solution.py:45
  51.9 2.4 %collective-permute-start.2 = (bf16[2,2,2,2,16,512]{5,4,3,2,1,0:T(8,128)(2,1)S(1)}, bf16[2,2,2,2,16,512]{5,4,3,2,1,0:T(8,128)(2,1)S(1)}, u32[]{:S(2)}, u32[]{:S(2)}) collective-permute-start(bf16[2,2,2,2,16,512]{5,4,3,2,1,0:T(8,128)(2,1)S(1)} %pad_maximum_fusion.3), channel_id=1, source_target_pairs={{0,64},{64,0},{1,65},{65,1},{2,66},{66,2},{3,67},{67,3},{4,68},{68... | collective-permute-start | bytes 786440 | tf_op jit(solution)/shard_map/ppermute | solution.py:45
  54.3 5.8 %collective-permute-done.2 = bf16[2,2,2,2,16,512]{5,4,3,2,1,0:T(8,128)(2,1)S(1)} collective-permute-done((bf16[2,2,2,2,16,512]{5,4,3,2,1,0:T(8,128)(2,1)S(1)}, bf16[2,2,2,2,16,512]{5,4,3,2,1,0:T(8,128)(2,1)S(1)}, u32[]{:S(2)}, u32[]{:S(2)}) %collective-permute-start.2) | collective-permute-done | bytes 262176 | tf_op jit(solution)/shard_map/ppermute | solution.py:45
  60.2 0.1 pad_maximum_fusion.1
  60.3 1.9 %collective-permute-start.3 = (bf16[2,2,2,2,2,16,512]{6,5,4,3,2,1,0:T(8,128)(2,1)S(1)}, bf16[2,2,2,2,2,16,512]{6,5,4,3,2,1,0:T(8,128)(2,1)S(1)}, u32[]{:S(2)}, u32[]{:S(2)}) collective-permute-start(bf16[2,2,2,2,2,16,512]{6,5,4,3,2,1,0:T(8,128)(2,1)S(1)} %pad_maximum_fusion.1), channel_id=1, source_target_pairs={{0,32},{32,0},{1,33},{33,1},{2,34},{34,2},{3,35},{35,3},{4,36},{36... | collective-permute-start | bytes 1572872 | tf_op jit(solution)/shard_map/ppermute | solution.py:45
  62.2 0.0 all-to-all-done.1
  62.2 1.3 convolution_convert_fusion.3
  63.5 8.5 %all-to-all-start.2 = ((bf16[16,32,512]{2,1,0:T(8,128)(2,1)}), bf16[16,32,512]{2,1,0:T(8,128)(2,1)S(1)}, u32[]{:S(2)}, u32[]{:S(2)}) async-start(bf16[16,32,512]{2,1,0:T(8,128)(2,1)} %bitcast.2), calls=%async_computation.2 | async-start | bytes 1048576 | tf_op jit(solution)/shard_map/all_to_all | solution.py:22
  72.0 0.0 collective-permute-done.3
  72.0 0.1 select_bitcast_fusion.1
  72.1 0.1 fusion.13
  72.2 10.5 %all-to-all-done.2 = bf16[16,32,512]{2,1,0:T(8,128)(2,1)S(1)} async-done(((bf16[16,32,512]{2,1,0:T(8,128)(2,1)}), bf16[16,32,512]{2,1,0:T(8,128)(2,1)S(1)}, u32[]{:S(2)}, u32[]{:S(2)}) %all-to-all-start.2) | async-done | bytes 524320 | tf_op jit(solution)/shard_map/all_to_all | solution.py:22
  82.7 0.1 reduce_sum.36
  82.8 0.7 broadcast_in_dim.34
  83.5 4.8 %all-to-all-start.3 = ((bf16[8,32,512]{2,1,0:T(8,128)(2,1)}), bf16[8,32,512]{2,1,0:T(8,128)(2,1)S(1)}, u32[]{:S(2)}, u32[]{:S(2)}) async-start(bf16[8,32,512]{2,1,0:T(8,128)(2,1)} %broadcast_in_dim.34), calls=%async_computation.3 | async-start | bytes 524288 | tf_op jit(solution)/shard_map/all_to_all | solution.py:22
  88.3 1.2 fusion.12
  89.5 7.3 %all-to-all-done.3 = bf16[8,32,512]{2,1,0:T(8,128)(2,1)S(1)} async-done(((bf16[8,32,512]{2,1,0:T(8,128)(2,1)}), bf16[8,32,512]{2,1,0:T(8,128)(2,1)S(1)}, u32[]{:S(2)}, u32[]{:S(2)}) %all-to-all-start.3) | async-done | bytes 262176 | tf_op jit(solution)/shard_map/all_to_all | solution.py:22
  96.8 2.2 %all-gather = bf16[16,32,512]{2,1,0:T(8,128)(2,1)S(1)} all-gather(bf16[8,32,512]{2,1,0:T(8,128)(2,1)S(1)} %all-to-all-done.3), channel_id=2, replica_groups=mesh['y_hi'=2,'x_hi'=2,'x_lo'=2,'core'=2,'y_lo'=2,'z3'=2,'z2'=2,'z1'=2,'..., dimensions={0}, use_global_device_ids=true | all-gather | bytes 786432 | tf_op jit(solution)/shard_map/all_gather | solution.py:73
  99.0 0.6 fusion.7
  99.6 0.4 copy-done.4
  100.0 0.5 fusion.14
  100.5 0.6 copy-done.1
  101.1 1.3 fusion
  102.3 3.8 %all-to-all-start.4 = ((bf16[4,8,16,512]{3,2,1,0:T(8,128)(2,1)}), bf16[4,8,16,512]{3,2,1,0:T(8,128)(2,1)S(1)}, u32[]{:S(2)}, u32[]{:S(2)}) async-start(bf16[4,8,16,512]{3,2,1,0:T(8,128)(2,1)} %bitcast.21), calls=%async_computation.4 | async-start | bytes 1048576 | tf_op jit(solution)/shard_map/all_to_all | solution.py:22
  106.1 3.9 %collective-permute-start.4 = (bf16[8,16,512]{2,1,0:T(8,128)(2,1)S(1)}, bf16[8,16,512]{2,1,0:T(8,128)(2,1)S(1)}, u32[]{:S(2)}, u32[]{:S(2)}) collective-permute-start(bf16[8,16,512]{2,1,0:T(8,128)(2,1)S(1)} %get-tuple-element.26), channel_id=1, source_target_pairs={{0,1},{1,0},{2,3},{3,2},{4,5},{5,4},{6,7},{7,6},{8,9},{9,8},{10,11... | collective-permute-start | bytes 393224 | tf_op jit(solution)/shard_map/ppermute | solution.py:45
  110.0 7.6 %collective-permute-done.4 = bf16[8,16,512]{2,1,0:T(8,128)(2,1)S(1)} collective-permute-done((bf16[8,16,512]{2,1,0:T(8,128)(2,1)S(1)}, bf16[8,16,512]{2,1,0:T(8,128)(2,1)S(1)}, u32[]{:S(2)}, u32[]{:S(2)}) %collective-permute-start.4) | collective-permute-done | bytes 131104 | tf_op jit(solution)/shard_map/ppermute | solution.py:45
  117.7 3.0 %collective-permute-start.5 = (bf16[2,8,16,512]{3,2,1,0:T(8,128)(2,1)S(1)}, bf16[2,8,16,512]{3,2,1,0:T(8,128)(2,1)S(1)}, u32[]{:S(2)}, u32[]{:S(2)}) collective-permute-start(bf16[2,8,16,512]{3,2,1,0:T(8,128)(2,1)S(1)} %pad_maximum_fusion.4), channel_id=1, source_target_pairs={{0,16},{16,0},{1,17},{17,1},{2,18},{18,2},{3,19},{19,3},{4,20},{20... | collective-permute-start | bytes 786440 | tf_op jit(solution)/shard_map/ppermute | solution.py:45
  120.7 6.6 %collective-permute-done.5 = bf16[2,8,16,512]{3,2,1,0:T(8,128)(2,1)S(1)} collective-permute-done((bf16[2,8,16,512]{3,2,1,0:T(8,128)(2,1)S(1)}, bf16[2,8,16,512]{3,2,1,0:T(8,128)(2,1)S(1)}, u32[]{:S(2)}, u32[]{:S(2)}) %collective-permute-start.5) | collective-permute-done | bytes 262176 | tf_op jit(solution)/shard_map/ppermute | solution.py:45
  127.3 0.0 copy-start.2
  127.3 0.8 pad_maximum_fusion.2
  128.1 0.4 copy-done.2
  128.5 1.3 convolution_convert_fusion
  129.8 0.0 all-to-all-done.4
  129.8 0.7 reduce_sum.37
  130.5 3.4 %all-to-all-start.5 = ((bf16[8,16,512]{2,1,0:T(8,128)(2,1)}), bf16[8,16,512]{2,1,0:T(8,128)(2,1)S(1)}, u32[]{:S(2)}, u32[]{:S(2)}) async-start(bf16[8,16,512]{2,1,0:T(8,128)(2,1)} %reduce_sum.37), calls=%async_computation.5 | async-start | bytes 262144 | tf_op jit(solution)/shard_map/all_to_all | solution.py:22
  133.9 1.3 convolution_convert_fusion.2
  135.2 1.3 convolution_convert_fusion.1
  136.4 11.8 %all-to-all-done.5 = bf16[8,16,512]{2,1,0:T(8,128)(2,1)S(1)} async-done(((bf16[8,16,512]{2,1,0:T(8,128)(2,1)}), bf16[8,16,512]{2,1,0:T(8,128)(2,1)S(1)}, u32[]{:S(2)}, u32[]{:S(2)}) %all-to-all-start.5) | async-done | bytes 131104 | tf_op jit(solution)/shard_map/all_to_all | solution.py:22
  148.2 0.6 reduce_sum.38
  (20 shorter events, 0.3 us)
Async XLA Ops:
  0.6 61.6 %copy-start = (bf16[512,512]{1,0:T(8,128)(2,1)S(1)}, bf16[512,512]{1,0:T(8,128)(2,1)}, u32[]{:S(2)}) copy-start(bf16[512,512]{1,0:T(8,128)(2,1)} %param.13) | copy-start | bytes 1572868
  2.2 15.2 %copy-start.5 = (bf16[32,512]{1,0:T(8,128)(2,1)S(1)}, bf16[32,512]{1,0:T(8,128)(2,1)}, u32[]{:S(2)}) copy-start(bf16[32,512]{1,0:T(8,128)(2,1)} %param.10) | copy-start | bytes 98308
  2.2 15.2 %copy-start.6 = (bf16[32,512]{1,0:T(8,128)(2,1)S(1)}, bf16[32,512]{1,0:T(8,128)(2,1)}, u32[]{:S(2)}) copy-start(bf16[32,512]{1,0:T(8,128)(2,1)} %param.9) | copy-start | bytes 98308
  2.2 36.6 %all-to-all-start = ((bf16[8,2,16,512]{3,2,1,0:T(8,128)(2,1)}), bf16[8,2,16,512]{3,2,1,0:T(8,128)(2,1)S(1)}, u32[]{:S(2)}, u32[]{:S(2)}) async-start(bf16[8,2,16,512]{3,2,1,0:T(8,128)(2,1)} %broadcast_select_fusion), calls=%async_computation | async-start | bytes 524288 | tf_op jit(solution)/shard_map/all_to_all | solution.py:22
  17.5 25.7 %collective-permute-start = (bf16[2,2,16,512]{3,2,1,0:T(8,128)(2,1)S(1)}, bf16[2,2,16,512]{3,2,1,0:T(8,128)(2,1)S(1)}, u32[]{:S(2)}, u32[]{:S(2)}) collective-permute-start(bf16[2,2,16,512]{3,2,1,0:T(8,128)(2,1)S(1)} %pad_maximum_fusion.6), channel_id=1, source_target_pairs={{0,256},{256,0},{1,257},{257,1},{2,258},{258,2},{3,259},{259,3},{4... | collective-permute-start | bytes 196616 | tf_op jit(solution)/shard_map/ppermute | solution.py:45
  39.7 22.5 %all-to-all-start.1 = ((bf16[4,8,16,512]{3,2,1,0:T(8,128)(2,1)}), bf16[4,8,16,512]{3,2,1,0:T(8,128)(2,1)S(1)}, u32[]{:S(2)}, u32[]{:S(2)}) async-start(bf16[4,8,16,512]{3,2,1,0:T(8,128)(2,1)} %broadcast_in_dim.33), calls=%async_computation.1 | async-start | bytes 1048576 | tf_op jit(solution)/shard_map/all_to_all | solution.py:22
  43.2 8.6 %collective-permute-start.1 = (bf16[2,2,2,16,512]{4,3,2,1,0:T(8,128)(2,1)S(1)}, bf16[2,2,2,16,512]{4,3,2,1,0:T(8,128)(2,1)S(1)}, u32[]{:S(2)}, u32[]{:S(2)}) collective-permute-start(bf16[2,2,2,16,512]{4,3,2,1,0:T(8,128)(2,1)S(1)} %pad_maximum_fusion.5), channel_id=1, source_target_pairs={{0,128},{128,0},{1,129},{129,1},{2,130},{130,2},{3,131},{131,3},{4... | collective-permute-start | bytes 393224 | tf_op jit(solution)/shard_map/ppermute | solution.py:45
  51.9 8.3 %collective-permute-start.2 = (bf16[2,2,2,2,16,512]{5,4,3,2,1,0:T(8,128)(2,1)S(1)}, bf16[2,2,2,2,16,512]{5,4,3,2,1,0:T(8,128)(2,1)S(1)}, u32[]{:S(2)}, u32[]{:S(2)}) collective-permute-start(bf16[2,2,2,2,16,512]{5,4,3,2,1,0:T(8,128)(2,1)S(1)} %pad_maximum_fusion.3), channel_id=1, source_target_pairs={{0,64},{64,0},{1,65},{65,1},{2,66},{66,2},{3,67},{67,3},{4,68},{68... | collective-permute-start | bytes 786440 | tf_op jit(solution)/shard_map/ppermute | solution.py:45
  60.3 11.8 %collective-permute-start.3 = (bf16[2,2,2,2,2,16,512]{6,5,4,3,2,1,0:T(8,128)(2,1)S(1)}, bf16[2,2,2,2,2,16,512]{6,5,4,3,2,1,0:T(8,128)(2,1)S(1)}, u32[]{:S(2)}, u32[]{:S(2)}) collective-permute-start(bf16[2,2,2,2,2,16,512]{6,5,4,3,2,1,0:T(8,128)(2,1)S(1)} %pad_maximum_fusion.1), channel_id=1, source_target_pairs={{0,32},{32,0},{1,33},{33,1},{2,34},{34,2},{3,35},{35,3},{4,36},{36... | collective-permute-start | bytes 1572872 | tf_op jit(solution)/shard_map/ppermute | solution.py:45
  63.5 19.3 %all-to-all-start.2 = ((bf16[16,32,512]{2,1,0:T(8,128)(2,1)}), bf16[16,32,512]{2,1,0:T(8,128)(2,1)S(1)}, u32[]{:S(2)}, u32[]{:S(2)}) async-start(bf16[16,32,512]{2,1,0:T(8,128)(2,1)} %bitcast.2), calls=%async_computation.2 | async-start | bytes 1048576 | tf_op jit(solution)/shard_map/all_to_all | solution.py:22
  83.5 13.3 %all-to-all-start.3 = ((bf16[8,32,512]{2,1,0:T(8,128)(2,1)}), bf16[8,32,512]{2,1,0:T(8,128)(2,1)S(1)}, u32[]{:S(2)}, u32[]{:S(2)}) async-start(bf16[8,32,512]{2,1,0:T(8,128)(2,1)} %broadcast_in_dim.34), calls=%async_computation.3 | async-start | bytes 524288 | tf_op jit(solution)/shard_map/all_to_all | solution.py:22
  99.0 1.0 copy-start.4
  100.0 1.0 copy-start.1
  102.3 27.5 %all-to-all-start.4 = ((bf16[4,8,16,512]{3,2,1,0:T(8,128)(2,1)}), bf16[4,8,16,512]{3,2,1,0:T(8,128)(2,1)S(1)}, u32[]{:S(2)}, u32[]{:S(2)}) async-start(bf16[4,8,16,512]{3,2,1,0:T(8,128)(2,1)} %bitcast.21), calls=%async_computation.4 | async-start | bytes 1048576 | tf_op jit(solution)/shard_map/all_to_all | solution.py:22
  106.1 11.5 %collective-permute-start.4 = (bf16[8,16,512]{2,1,0:T(8,128)(2,1)S(1)}, bf16[8,16,512]{2,1,0:T(8,128)(2,1)S(1)}, u32[]{:S(2)}, u32[]{:S(2)}) collective-permute-start(bf16[8,16,512]{2,1,0:T(8,128)(2,1)S(1)} %get-tuple-element.26), channel_id=1, source_target_pairs={{0,1},{1,0},{2,3},{3,2},{4,5},{5,4},{6,7},{7,6},{8,9},{9,8},{10,11... | collective-permute-start | bytes 393224 | tf_op jit(solution)/shard_map/ppermute | solution.py:45
  117.7 9.5 %collective-permute-start.5 = (bf16[2,8,16,512]{3,2,1,0:T(8,128)(2,1)S(1)}, bf16[2,8,16,512]{3,2,1,0:T(8,128)(2,1)S(1)}, u32[]{:S(2)}, u32[]{:S(2)}) collective-permute-start(bf16[2,8,16,512]{3,2,1,0:T(8,128)(2,1)S(1)} %pad_maximum_fusion.4), channel_id=1, source_target_pairs={{0,16},{16,0},{1,17},{17,1},{2,18},{18,2},{3,19},{19,3},{4,20},{20... | collective-permute-start | bytes 786440 | tf_op jit(solution)/shard_map/ppermute | solution.py:45
  127.3 1.2 copy-start.2
  129.8 4.1 %copy-start.3 = (bf16[2,2,8,16,512]{4,3,2,1,0:T(8,128)(2,1)S(1)}, bf16[2,2,8,16,512]{4,3,2,1,0:T(8,128)(2,1)}, u32[]{:S(2)}) copy-start(bf16[2,2,8,16,512]{4,3,2,1,0:T(8,128)(2,1)} %pad_maximum_fusion.2) | copy-start | bytes 1572868
  130.5 17.7 %all-to-all-start.5 = ((bf16[8,16,512]{2,1,0:T(8,128)(2,1)}), bf16[8,16,512]{2,1,0:T(8,128)(2,1)S(1)}, u32[]{:S(2)}, u32[]{:S(2)}) async-start(bf16[8,16,512]{2,1,0:T(8,128)(2,1)} %reduce_sum.37), calls=%async_computation.5 | async-start | bytes 262144 | tf_op jit(solution)/shard_map/all_to_all | solution.py:22
